TPU v7x, 512 devices: a whole 4x8x8 slice. The times are simulated.
512 devices in a mesh: tm: 64 (over x, y, core), dp: 8 (over z).
Axes of the slice: x: 4, y: 8, z: 8, core: 2. Of those that a mesh axis runs over, the one named last changes fastest.
Arguments:
- frame_tokens: bfloat16 [8, 192, 64, 1280], P('dp', 'tm'), may hold values from -8 to 8
- visible: int32 [8, 192, 64], P('dp'), may hold values from 0 to 2
- grad_output: bfloat16 [8, 192, 64, 1280], P('dp', 'tm'), may hold values from -16 to 16
- norm_gain: float32 [1280], replicated, may hold values from 0.1 to 1.9
- query_weight: bfloat16 [1280, 640], P('tm'), may hold values from -1.5 to 1.5
- key_weight: bfloat16 [1280, 640], P('tm'), may hold values from -1.5 to 1.5
- value_weight: bfloat16 [1280, 640], P('tm'), may hold values from -0.15625 to 0.15625
- output_weight: bfloat16 [640, 1280], P('tm'), may hold values from -0.25 to 0.25
Outputs:
- block_out: bfloat16 [8, 192, 64, 1280], P('dp', 'tm')
- grad_tokens: bfloat16 [8, 192, 64, 1280], P('dp', 'tm')
- grad_output_weight: float32 [640, 1280], P('tm')
Inputs may be any that keep to these rules, and one draw needn't show every extreme that they name: visible[c, f, g] names which of the 3 cells of group g is visible in frame f.
All inputs are finite; a program needn't handle non-finite values.
Results may differ from a plain program's by a relative error of at most 0.012.
Values may be sent and summed in bfloat16 or wider, within the bound.
No kernel may reach another device: no remote copies, remote signals or barrier semaphores. Data moves between devices by JAX's collectives and lax.ppermute only.
A program may use at most 64 MiB of HBM per device.

v0:
```python
import math
import jax
import jax.numpy as jnp
from jax import lax
from jax.sharding import PartitionSpec as P

HEADS = 8
NORM_EPS = 1e-06


def normalize(token_rows, norm_gain):
    values = token_rows.astype(jnp.float32)
    centered = values - jnp.mean(values, axis=-1, keepdims=True)
    inverse = lax.rsqrt(jnp.mean(centered * centered, axis=-1, keepdims=True) + NORM_EPS)
    scaled = centered * inverse
    return (scaled, inverse, (scaled * norm_gain).astype(jnp.bfloat16))


def project(token_rows, weight):
    lead_shape = token_rows.shape[:-1]
    flat_rows = token_rows.reshape(-1, token_rows.shape[-1])
    result = jnp.dot(flat_rows, weight, preferred_element_type=jnp.float32)
    return result.astype(jnp.bfloat16).reshape(lead_shape + (weight.shape[1],))


def split_heads(values):
    return values.reshape(values.shape[:-1] + (HEADS, values.shape[-1] // HEADS))


def attend(query_rows, key_rows, value_rows, same_cell):
    score_scale = 1.0 / math.sqrt(query_rows.shape[-1] // HEADS)
    query_heads = split_heads(query_rows)
    key_heads = split_heads(key_rows)
    value_heads = split_heads(value_rows)
    scores = (
        jnp.einsum("fghe,tghe->ghft", query_heads, key_heads, preferred_element_type=jnp.float32)
        * score_scale
    )
    scores = jnp.where(same_cell[:, None], scores, -jnp.inf)
    row_top = jnp.max(scores, axis=-1, keepdims=True)
    expons = jnp.exp(scores - row_top)
    soft_probs = expons / jnp.sum(expons, axis=-1, keepdims=True)
    probs_low = soft_probs.astype(jnp.bfloat16)
    mixed_rows = jnp.einsum(
        "ghft,tghe->fghe", probs_low, value_heads, preferred_element_type=jnp.float32
    )
    return (soft_probs, probs_low, mixed_rows.reshape(query_rows.shape).astype(jnp.bfloat16))


def attend_back(query_rows, key_rows, value_rows, soft_probs, probs_low, grad_mixed):
    score_scale = 1.0 / math.sqrt(query_rows.shape[-1] // HEADS)
    query_heads = split_heads(query_rows)
    key_heads = split_heads(key_rows)
    value_heads = split_heads(value_rows)
    grad_heads = split_heads(grad_mixed)
    grad_probs = jnp.einsum(
        "fghe,tghe->ghft", grad_heads, value_heads, preferred_element_type=jnp.float32
    )
    centre = jnp.sum(soft_probs * grad_probs, axis=-1, keepdims=True)
    grad_scores = (soft_probs * (grad_probs - centre) * score_scale).astype(jnp.bfloat16)
    grad_query = jnp.einsum(
        "ghft,tghe->fghe", grad_scores, key_heads, preferred_element_type=jnp.float32
    )
    grad_key = jnp.einsum(
        "ghft,fghe->tghe", grad_scores, query_heads, preferred_element_type=jnp.float32
    )
    grad_value = jnp.einsum(
        "ghft,fghe->tghe", probs_low, grad_heads, preferred_element_type=jnp.float32
    )
    full_shape = query_rows.shape
    return (
        grad_query.reshape(full_shape).astype(jnp.bfloat16),
        grad_key.reshape(full_shape).astype(jnp.bfloat16),
        grad_value.reshape(full_shape).astype(jnp.bfloat16),
    )


def back_project(grad_query, grad_key, grad_value, query_weight, key_weight, value_weight):
    lead_shape = grad_query.shape[:-1]
    width = grad_query.shape[-1]
    total = jnp.dot(
        grad_query.reshape(-1, width), query_weight.T, preferred_element_type=jnp.float32
    )
    total = total + jnp.dot(
        grad_key.reshape(-1, width), key_weight.T, preferred_element_type=jnp.float32
    )
    total = total + jnp.dot(
        grad_value.reshape(-1, width), value_weight.T, preferred_element_type=jnp.float32
    )
    return total.astype(jnp.bfloat16).reshape(lead_shape + (query_weight.shape[0],))


def on_device(
    frame_tokens,
    visible,
    grad_output,
    norm_gain,
    query_weight,
    key_weight,
    value_weight,
    output_weight,
):
    query_weight, key_weight, value_weight, output_weight = (
        lax.all_gather(query_weight, "tm", axis=0, tiled=True),
        lax.all_gather(key_weight, "tm", axis=0, tiled=True),
        lax.all_gather(value_weight, "tm", axis=0, tiled=True),
        lax.all_gather(output_weight, "tm", axis=0, tiled=True),
    )
    shards = lax.axis_size("tm")
    tokens = frame_tokens[0]
    frame_count, visible_count, width = tokens.shape
    att_width = output_weight.shape[0]
    groups = visible_count // shards
    scaled, inverse, normed = normalize(tokens, norm_gain)
    local_cells = lax.dynamic_slice_in_dim(visible[0], lax.axis_index("tm") * groups, groups, 1)
    cell_major = local_cells.T
    same_cell = cell_major[:, :, None] == cell_major[:, None, :]
    query_rows = project(normed, query_weight)
    key_rows = project(normed, key_weight)
    value_rows = project(normed, value_weight)
    query_rows, key_rows, value_rows = (
        lax.all_to_all(query_rows, "tm", split_axis=1, concat_axis=0, tiled=True),
        lax.all_to_all(key_rows, "tm", split_axis=1, concat_axis=0, tiled=True),
        lax.all_to_all(value_rows, "tm", split_axis=1, concat_axis=0, tiled=True),
    )
    soft_probs, probs_low, mixed_cells = attend(query_rows, key_rows, value_rows, same_cell)
    mixed_frames = lax.all_to_all(mixed_cells, "tm", split_axis=0, concat_axis=1, tiled=True)
    flat_mixed = mixed_frames.reshape(-1, att_width)
    flat_tokens = tokens.reshape(-1, width)
    update = jnp.dot(flat_mixed, output_weight, preferred_element_type=jnp.float32)
    block_rows = (
        (flat_tokens.astype(jnp.float32) + update).astype(jnp.bfloat16).reshape(tokens.shape)
    )
    flat_grad = grad_output[0].reshape(-1, width)
    grad_mixed = jnp.dot(flat_grad, output_weight.T, preferred_element_type=jnp.float32)
    grad_mixed = grad_mixed.astype(jnp.bfloat16).reshape(frame_count, visible_count, att_width)
    term_share = lax.psum_scatter(
        jnp.dot(flat_mixed.T, flat_grad, preferred_element_type=jnp.float32),
        "tm",
        scatter_dimension=0,
        tiled=True,
    )
    grad_weight = lax.psum(term_share.astype(jnp.bfloat16), "dp").astype(jnp.float32)
    grad_cells = lax.all_to_all(grad_mixed, "tm", split_axis=1, concat_axis=0, tiled=True)
    grad_query, grad_key, grad_value = attend_back(
        query_rows, key_rows, value_rows, soft_probs, probs_low, grad_cells
    )
    grad_query, grad_key, grad_value = (
        lax.all_to_all(grad_query, "tm", split_axis=0, concat_axis=1, tiled=True),
        lax.all_to_all(grad_key, "tm", split_axis=0, concat_axis=1, tiled=True),
        lax.all_to_all(grad_value, "tm", split_axis=0, concat_axis=1, tiled=True),
    )
    grad_normed = back_project(
        grad_query, grad_key, grad_value, query_weight, key_weight, value_weight
    )
    weighted = grad_normed.astype(jnp.float32) * norm_gain
    first_mean = jnp.mean(weighted, axis=-1, keepdims=True)
    second_mean = jnp.mean(weighted * scaled, axis=-1, keepdims=True)
    grad_rows = inverse * (weighted - first_mean - scaled * second_mean) + grad_output[0].astype(
        jnp.float32
    )
    return (block_rows[None], grad_rows.astype(jnp.bfloat16)[None], grad_weight)


def solution(mesh):
    return jax.shard_map(
        on_device,
        mesh=mesh,
        in_specs=(
            P("dp", "tm", None, None),
            P("dp", None, None),
            P("dp", "tm", None, None),
            P(),
            P("tm", None),
            P("tm", None),
            P("tm", None),
            P("tm", None),
        ),
        out_specs=(P("dp", "tm", None, None), P("dp", "tm", None, None), P("tm", None)),
        check_vma=False,
    )
```

profile of v0, /device:TPU:64, one launch (start us, length us, event | category | flops | bytes accessed | tf_op | source)
XLA Modules:
  0.0 840.5 jit_solution(8921300924261810447)
XLA Ops:
  12.6 85.6 %all-gather.15.cloned.1.call-done = bf16[64,10,1280]{2,1,0:T(8,128)(2,1)} async-done(((bf16[1,10,1280]{2,1,0:T(8,128)(2,1)}), bf16[64,10,1280]{2,1,0:T(8,128)(2,1)}) %all-gather.15.cloned.1.call-update) | async-done | bytes 1638416 | tf_op jit(solution)/shard_map/all_gather | solution.py:107
  102.6 6.7 all-to-all-start.4
  110.7 71.2 %all-gather.13.cloned.1.call-done = bf16[64,20,640]{2,1,0:T(8,128)(2,1)} async-done(((bf16[1,20,640]{2,1,0:T(8,128)(2,1)}), bf16[64,20,640]{2,1,0:T(8,128)(2,1)}) %all-gather.13.cloned.1.call-update) | async-done | bytes 1638416 | tf_op jit(solution)/shard_map/all_gather | solution.py:105
  185.9 7.0 all-to-all-start.2
  192.9 72.7 %all-gather.11.cloned.1.call-done = bf16[64,20,640]{2,1,0:T(8,128)(2,1)} async-done(((bf16[1,20,640]{2,1,0:T(8,128)(2,1)}), bf16[64,20,640]{2,1,0:T(8,128)(2,1)}) %all-gather.11.cloned.1.call-update) | async-done | bytes 1638416 | tf_op jit(solution)/shard_map/all_gather | solution.py:104
  270.7 7.0 all-to-all-start.1
  277.8 71.5 %all-gather.9.cloned.1.call-done = bf16[64,20,640]{2,1,0:T(8,128)(2,1)} async-done(((bf16[1,20,640]{2,1,0:T(8,128)(2,1)}), bf16[64,20,640]{2,1,0:T(8,128)(2,1)}) %all-gather.9.cloned.1.call-update) | async-done | bytes 1638416 | tf_op jit(solution)/shard_map/all_gather | solution.py:106
  349.3 3.6 reshape.310
  364.3 7.0 all-to-all-start
  375.5 2.9 fusion.42
  387.9 10.7 %all-to-all-start.7 = ((bf16[64,2,960]{2,1,0:T(2,128)(2,1)}), bf16[64,2,960]{2,1,0:T(2,128)(2,1)}, u32[]{:S(2)}, u32[]{:S(2)}) async-start(bf16[64,2,960]{2,1,0:T(2,128)(2,1)} %reshape.328), calls=%async_computation.7 | async-start | bytes 524288 | tf_op jit(solution)/shard_map/all_to_all | solution.py:151
  411.6 10.5 %all-to-all-start.3 = ((bf16[64,2,960]{2,1,0:T(2,128)(2,1)}), bf16[64,2,960]{2,1,0:T(2,128)(2,1)}, u32[]{:S(2)}, u32[]{:S(2)}) async-start(bf16[64,2,960]{2,1,0:T(2,128)(2,1)} %reshape.322), calls=%async_computation.3 | async-start | bytes 524288 | tf_op jit(solution)/shard_map/all_to_all | solution.py:127
  424.7 4.3 fusion.19
  435.3 10.5 %all-to-all-start.6 = ((bf16[64,2,960]{2,1,0:T(2,128)(2,1)}), bf16[64,2,960]{2,1,0:T(2,128)(2,1)}, u32[]{:S(2)}, u32[]{:S(2)}) async-start(bf16[64,2,960]{2,1,0:T(2,128)(2,1)} %reshape.326), calls=%async_computation.6 | async-start | bytes 524288 | tf_op jit(solution)/shard_map/all_to_all | solution.py:150
  447.8 4.4 fusion.16
  461.3 3.1 reduce.12
  470.7 3.1 reduce.9
  477.2 10.5 %all-to-all-start.5 = ((bf16[64,2,960]{2,1,0:T(2,128)(2,1)}), bf16[64,2,960]{2,1,0:T(2,128)(2,1)}, u32[]{:S(2)}, u32[]{:S(2)}) async-start(bf16[64,2,960]{2,1,0:T(2,128)(2,1)} %reshape.324), calls=%async_computation.5 | async-start | bytes 524288 | tf_op jit(solution)/shard_map/all_to_all | solution.py:149
  487.7 2.9 reshape.327
  490.6 3.1 reduce.11
  497.1 3.0 fusion.2
  505.3 3.1 reduce.10
  514.9 287.3 %all-reduce.2 = bf16[640,1280]{1,0:T(8,128)(2,1)} all-reduce(f32[640,1280]{1,0:T(8,128)} %fusion.45), channel_id=2, replica_groups=mesh['tm'=64,'dp'=8] {'tm'}, use_global_device_ids=true, to_apply=%region_7.8.clone | all-reduce | flops 819200 | bytes 4915200
  803.0 29.0 %psum.7 = bf16[10,1280]{1,0:T(8,128)(2,1)S(1)} all-reduce(bf16[10,1280]{1,0:T(8,128)(2,1)S(1)} %dynamic-slice_convert_fusion), channel_id=1, replica_groups=mesh['tm'=64,'dp'=8] {'dp'}, use_global_device_ids=true, to_apply=%region_8.9 | all-reduce | flops 12800 | bytes 51200 | tf_op jit(solution)/shard_map/psum | solution.py:143
  (112 shorter events, 105.1 us)
Async XLA Ops:
  7.2 185.7 %copy-start = (s32[1,192,64]{1,2,0:T(8,128)S(1)}, s32[1,192,64]{1,2,0:T(8,128)}, u32[]{:S(2)}) copy-start(s32[1,192,64]{1,2,0:T(8,128)} %param.9) | copy-start | bytes 147460
  7.2 91.1 %all-gather.15.cloned.1.call-start = ((), (), s32[]{:S(2)}) async-start(), calls=%async_computation.11 | async-start | bytes 2662400 | tf_op jit(solution)/shard_map/all_gather | solution.py:107
  7.9 174.0 %all-gather.13.cloned.1.call-start = ((), (), s32[]{:S(2)}) async-start(), calls=%async_computation.10 | async-start | bytes 1996800 | tf_op jit(solution)/shard_map/all_gather | solution.py:105
  8.7 257.0 %all-gather.11.cloned.1.call-start = ((), (), s32[]{:S(2)}) async-start(), calls=%async_computation.9 | async-start | bytes 1996800 | tf_op jit(solution)/shard_map/all_gather | solution.py:104
  9.4 339.9 %all-gather.9.cloned.1.call-start = ((), (), s32[]{:S(2)}) async-start(), calls=%async_computation.8 | async-start | bytes 1996800 | tf_op jit(solution)/shard_map/all_gather | solution.py:106
  12.6 88.3 %copy-start.6 = (bf16[1,3,64,1280]{3,2,1,0:T(8,128)(2,1)S(1)}, bf16[1,3,64,1280]{3,2,1,0:T(8,128)(2,1)}, u32[]{:S(2)}) copy-start(bf16[1,3,64,1280]{3,2,1,0:T(8,128)(2,1)} %param.10) | copy-start | bytes 1474564
  101.0 8.4 copy-start.3
  101.0 8.4 copy-start.14
  102.6 83.2 %all-to-all-start.4 = ((bf16[3,64,640]{2,0,1:T(4,128)(2,1)}), bf16[3,64,640]{2,0,1:T(4,128)(2,1)S(1)}, u32[]{:S(2)}, u32[]{:S(2)}) async-start(bf16[3,64,640]{2,0,1:T(4,128)(2,1)} %copy.52), calls=%async_computation.4 | async-start | bytes 655360 | tf_op jit(solution)/shard_map/all_to_all | solution.py:144
  110.7 73.6 %copy-start.5 = (bf16[192,1280]{1,0:T(8,128)(2,1)}, bf16[192,1280]{1,0:T(8,128)(2,1)S(1)}, u32[]{:S(2)}) copy-start(bf16[192,1280]{1,0:T(8,128)(2,1)S(1)} %get-tuple-element.6) | copy-start | bytes 1474564
  185.9 7.1 copy-start.11
  185.9 84.8 %all-to-all-start.2 = ((bf16[3,64,640]{2,0,1:T(4,128)(2,1)}), bf16[3,64,640]{2,0,1:T(4,128)(2,1)}, u32[]{:S(2)}, u32[]{:S(2)}) async-start(bf16[3,64,640]{2,0,1:T(4,128)(2,1)} %copy.45), calls=%async_computation.2 | async-start | bytes 655360 | tf_op jit(solution)/shard_map/all_to_all | solution.py:123
  270.7 93.7 %all-to-all-start.1 = ((bf16[3,64,640]{2,0,1:T(4,128)(2,1)}), bf16[3,64,640]{2,0,1:T(4,128)(2,1)}, u32[]{:S(2)}, u32[]{:S(2)}) async-start(bf16[3,64,640]{2,0,1:T(4,128)(2,1)} %copy.44), calls=%async_computation.1 | async-start | bytes 655360 | tf_op jit(solution)/shard_map/all_to_all | solution.py:122
  364.3 23.6 %all-to-all-start = ((bf16[3,64,640]{2,0,1:T(4,128)(2,1)}), bf16[3,64,640]{2,0,1:T(4,128)(2,1)}, u32[]{:S(2)}, u32[]{:S(2)}) async-start(bf16[3,64,640]{2,0,1:T(4,128)(2,1)} %copy.43), calls=%async_computation | async-start | bytes 655360 | tf_op jit(solution)/shard_map/all_to_all | solution.py:124
  387.9 23.7 %all-to-all-start.7 = ((bf16[64,2,960]{2,1,0:T(2,128)(2,1)}), bf16[64,2,960]{2,1,0:T(2,128)(2,1)}, u32[]{:S(2)}, u32[]{:S(2)}) async-start(bf16[64,2,960]{2,1,0:T(2,128)(2,1)} %reshape.328), calls=%async_computation.7 | async-start | bytes 524288 | tf_op jit(solution)/shard_map/all_to_all | solution.py:151
  411.6 23.8 %all-to-all-start.3 = ((bf16[64,2,960]{2,1,0:T(2,128)(2,1)}), bf16[64,2,960]{2,1,0:T(2,128)(2,1)}, u32[]{:S(2)}, u32[]{:S(2)}) async-start(bf16[64,2,960]{2,1,0:T(2,128)(2,1)} %reshape.322), calls=%async_computation.3 | async-start | bytes 524288 | tf_op jit(solution)/shard_map/all_to_all | solution.py:127
  435.3 41.9 %all-to-all-start.6 = ((bf16[64,2,960]{2,1,0:T(2,128)(2,1)}), bf16[64,2,960]{2,1,0:T(2,128)(2,1)}, u32[]{:S(2)}, u32[]{:S(2)}) async-start(bf16[64,2,960]{2,1,0:T(2,128)(2,1)} %reshape.326), calls=%async_computation.6 | async-start | bytes 524288 | tf_op jit(solution)/shard_map/all_to_all | solution.py:150
  477.2 25.3 %all-to-all-start.5 = ((bf16[64,2,960]{2,1,0:T(2,128)(2,1)}), bf16[64,2,960]{2,1,0:T(2,128)(2,1)}, u32[]{:S(2)}, u32[]{:S(2)}) async-start(bf16[64,2,960]{2,1,0:T(2,128)(2,1)} %reshape.324), calls=%async_computation.5 | async-start | bytes 524288 | tf_op jit(solution)/shard_map/all_to_all | solution.py:149
  497.1 3.0 copy-start.7
  497.1 3.0 copy-start.10
  512.1 1.7 copy-start.9
  512.1 1.7 copy-start.12
  514.9 317.8 %copy-start.4 = (bf16[1,3,64,1280]{3,2,1,0:T(8,128)(2,1)S(1)}, bf16[1,3,64,1280]{3,2,1,0:T(8,128)(2,1)}, u32[]{:S(2)}) copy-start(bf16[1,3,64,1280]{3,2,1,0:T(8,128)(2,1)} %param.8) | copy-start | bytes 1474564
  514.9 317.8 %copy-start.8 = (bf16[1,3,64,1280]{3,2,1,0:T(8,128)(2,1)S(1)}, bf16[1,3,64,1280]{3,2,1,0:T(8,128)(2,1)}, u32[]{:S(2)}) copy-start(bf16[1,3,64,1280]{3,2,1,0:T(8,128)(2,1)} %param.10) | copy-start | bytes 1474564
  (3 other events, 4.0 us)
Sparse Core Ops, SparseCore 0:
  11.3 86.8 all-gather.14
  101.5 80.3 all-gather.12
  185.2 80.4 all-gather.10
  268.8 80.4 all-gather.8
where the time goes:
time: 843 us; the launch traced here: 840 us
  blocking collectives  316 us (37%)
  waiting for transfers between devices  304 us (36%)
  local copies, waits for them, and re-layouts  75.6 us (9%)
  starting transfers between devices  70.1 us (8%)
  matrix products  31.9 us (4%)
  other arithmetic  28.2 us (3%)
  between operations  14.7 us (2%)
    unnamed x1, blocking collectives  287 us
    all_gather x1, waiting for transfers between devices, on_device(): lax.all_gather(output_weight, 'tm', axis=0, tiled=True)  85.6 us
    all_gather x1, waiting for transfers between devices, on_device(): lax.all_gather(query_weight, 'tm', axis=0, tiled=True)  72.7 us
    all_gather x1, waiting for transfers between devices, on_device(): lax.all_gather(value_weight, 'tm', axis=0, tiled=True)  71.5 us
    all_gather x1, waiting for transfers between devices, on_device(): lax.all_gather(key_weight, 'tm', axis=0, tiled=True)  71.2 us
    unnamed x47, local copies, waits for them, and re-layouts  40.3 us
    psum x1, blocking collectives, on_device(): lax.psum(term_share.astype(jnp.bfloat16), 'dp').astype(jnp.float32)  29 us
  transfers between devices with their start and end apart: 12, of which 4 were waited for; matrix products, arithmetic and copies ran while one was open for 14% of the time, Pallas kernels for 0%

commit v1 on v0

--- a/solution.py
+++ b/solution.py
@@ -140,7 +140,9 @@
         scatter_dimension=0,
         tiled=True,
     )
-    grad_weight = lax.psum(term_share.astype(jnp.bfloat16), "dp").astype(jnp.float32)
+    grad_weight = jnp.sum(lax.all_gather(term_share.astype(jnp.bfloat16), "dp"), axis=0).astype(
+        jnp.float32
+    )
     grad_cells = lax.all_to_all(grad_mixed, "tm", split_axis=1, concat_axis=0, tiled=True)
     grad_query, grad_key, grad_value = attend_back(
         query_rows, key_rows, value_rows, soft_probs, probs_low, grad_cells

time: 843 us -> 840 us (level)
    psum x1 -> x0, blocking collectives: 29 us -> none  [on_device(): lax.psum(term_share.astype(jnp.bfloat16), 'dp').astype(jnp.float32)]
    all_gather x0 -> x1, blocking collectives: none -> 26 us  [on_device(): lax.all_gather(term_share.astype(jnp.bfloat16), 'dp')]
    unnamed x47 -> x48, local copies, waits for them, and re-layouts: 40.3 us -> 41.2 us
where the time goes in v1:
time: 840 us; the launch traced here: 838 us
  blocking collectives  313 us (37%)
  waiting for transfers between devices  304 us (36%)
  local copies, waits for them, and re-layouts  75.6 us (9%)
  starting transfers between devices  70.1 us (8%)
  matrix products  31.9 us (4%)
  other arithmetic  28.3 us (3%)
  between operations  14.7 us (2%)
    unnamed x1, blocking collectives  287 us
    all_gather x1, waiting for transfers between devices, on_device(): lax.all_gather(output_weight, 'tm', axis=0, tiled=True)  85.6 us
    all_gather x1, waiting for transfers between devices, on_device(): lax.all_gather(query_weight, 'tm', axis=0, tiled=True)  72.7 us
    all_gather x1, waiting for transfers between devices, on_device(): lax.all_gather(value_weight, 'tm', axis=0, tiled=True)  71.5 us
    all_gather x1, waiting for transfers between devices, on_device(): lax.all_gather(key_weight, 'tm', axis=0, tiled=True)  71.2 us
    unnamed x48, local copies, waits for them, and re-layouts  41.2 us
    all_gather x1, blocking collectives, on_device(): lax.all_gather(term_share.astype(jnp.bfloat16), 'dp')  26 us
  transfers between devices with their start and end apart: 12, of which 4 were waited for; matrix products, arithmetic and copies ran while one was open for 14% of the time, Pallas kernels for 0%

profile of v1, /device:TPU:64, one launch (start us, length us, event | category | flops | bytes accessed | tf_op | source)
XLA Modules:
  0.0 837.5 jit_solution(13185301400653772636)
XLA Ops:
  12.6 85.6 %all-gather.17.cloned.1.call-done = bf16[64,10,1280]{2,1,0:T(8,128)(2,1)} async-done(((bf16[1,10,1280]{2,1,0:T(8,128)(2,1)}), bf16[64,10,1280]{2,1,0:T(8,128)(2,1)}) %all-gather.17.cloned.1.call-update) | async-done | bytes 1638416 | tf_op jit(solution)/shard_map/all_gather | solution.py:107
  102.6 6.7 all-to-all-start.4
  110.7 71.2 %all-gather.15.cloned.1.call-done = bf16[64,20,640]{2,1,0:T(8,128)(2,1)} async-done(((bf16[1,20,640]{2,1,0:T(8,128)(2,1)}), bf16[64,20,640]{2,1,0:T(8,128)(2,1)}) %all-gather.15.cloned.1.call-update) | async-done | bytes 1638416 | tf_op jit(solution)/shard_map/all_gather | solution.py:105
  185.9 7.0 all-to-all-start.2
  192.9 72.7 %all-gather.13.cloned.1.call-done = bf16[64,20,640]{2,1,0:T(8,128)(2,1)} async-done(((bf16[1,20,640]{2,1,0:T(8,128)(2,1)}), bf16[64,20,640]{2,1,0:T(8,128)(2,1)}) %all-gather.13.cloned.1.call-update) | async-done | bytes 1638416 | tf_op jit(solution)/shard_map/all_gather | solution.py:104
  270.7 7.0 all-to-all-start.1
  277.8 71.5 %all-gather.11.cloned.1.call-done = bf16[64,20,640]{2,1,0:T(8,128)(2,1)} async-done(((bf16[1,20,640]{2,1,0:T(8,128)(2,1)}), bf16[64,20,640]{2,1,0:T(8,128)(2,1)}) %all-gather.11.cloned.1.call-update) | async-done | bytes 1638416 | tf_op jit(solution)/shard_map/all_gather | solution.py:106
  349.3 3.6 reshape.311
  364.3 7.0 all-to-all-start
  375.5 2.9 fusion.43
  387.9 10.7 %all-to-all-start.7 = ((bf16[64,2,960]{2,1,0:T(2,128)(2,1)}), bf16[64,2,960]{2,1,0:T(2,128)(2,1)}, u32[]{:S(2)}, u32[]{:S(2)}) async-start(bf16[64,2,960]{2,1,0:T(2,128)(2,1)} %reshape.332), calls=%async_computation.7 | async-start | bytes 524288 | tf_op jit(solution)/shard_map/all_to_all | solution.py:153
  411.6 10.5 %all-to-all-start.3 = ((bf16[64,2,960]{2,1,0:T(2,128)(2,1)}), bf16[64,2,960]{2,1,0:T(2,128)(2,1)}, u32[]{:S(2)}, u32[]{:S(2)}) async-start(bf16[64,2,960]{2,1,0:T(2,128)(2,1)} %reshape.326), calls=%async_computation.3 | async-start | bytes 524288 | tf_op jit(solution)/shard_map/all_to_all | solution.py:127
  424.7 4.3 fusion.19
  435.3 10.5 %all-to-all-start.6 = ((bf16[64,2,960]{2,1,0:T(2,128)(2,1)}), bf16[64,2,960]{2,1,0:T(2,128)(2,1)}, u32[]{:S(2)}, u32[]{:S(2)}) async-start(bf16[64,2,960]{2,1,0:T(2,128)(2,1)} %reshape.330), calls=%async_computation.6 | async-start | bytes 524288 | tf_op jit(solution)/shard_map/all_to_all | solution.py:152
  447.8 4.4 fusion.16
  461.3 3.1 reduce.14
  470.7 3.1 reduce.11
  477.2 10.5 %all-to-all-start.5 = ((bf16[64,2,960]{2,1,0:T(2,128)(2,1)}), bf16[64,2,960]{2,1,0:T(2,128)(2,1)}, u32[]{:S(2)}, u32[]{:S(2)}) async-start(bf16[64,2,960]{2,1,0:T(2,128)(2,1)} %reshape.328), calls=%async_computation.5 | async-start | bytes 524288 | tf_op jit(solution)/shard_map/all_to_all | solution.py:151
  487.7 2.9 reshape.331
  490.6 3.1 reduce.13
  497.1 3.0 fusion.2
  505.3 3.1 reduce.12
  514.9 287.3 %all-reduce.2 = bf16[640,1280]{1,0:T(8,128)(2,1)} all-reduce(f32[640,1280]{1,0:T(8,128)} %fusion.46), channel_id=3, replica_groups=mesh['tm'=64,'dp'=8] {'tm'}, use_global_device_ids=true, to_apply=%region_7.8.clone | all-reduce | flops 819200 | bytes 4915200
  803.0 26.0 %all-gather.5 = bf16[8,10,1280]{2,1,0:T(8,128)(2,1)S(1)} all-gather(bf16[1,10,1280]{2,1,0:T(8,128)(2,1)S(1)} %fusion.35), channel_id=2, replica_groups=mesh['tm'=64,'dp'=8] {'dp'}, dimensions={0}, use_global_device_ids=true | all-gather | bytes 230400 | tf_op jit(solution)/shard_map/all_gather | solution.py:143
  (113 shorter events, 105.2 us)
Async XLA Ops:
  7.2 185.7 %copy-start = (s32[1,192,64]{1,2,0:T(8,128)S(1)}, s32[1,192,64]{1,2,0:T(8,128)}, u32[]{:S(2)}) copy-start(s32[1,192,64]{1,2,0:T(8,128)} %param.9) | copy-start | bytes 147460
  7.2 91.1 %all-gather.17.cloned.1.call-start = ((), (), s32[]{:S(2)}) async-start(), calls=%async_computation.11 | async-start | bytes 2662400 | tf_op jit(solution)/shard_map/all_gather | solution.py:107
  7.9 174.0 %all-gather.15.cloned.1.call-start = ((), (), s32[]{:S(2)}) async-start(), calls=%async_computation.10 | async-start | bytes 1996800 | tf_op jit(solution)/shard_map/all_gather | solution.py:105
  8.7 257.0 %all-gather.13.cloned.1.call-start = ((), (), s32[]{:S(2)}) async-start(), calls=%async_computation.9 | async-start | bytes 1996800 | tf_op jit(solution)/shard_map/all_gather | solution.py:104
  9.4 339.9 %all-gather.11.cloned.1.call-start = ((), (), s32[]{:S(2)}) async-start(), calls=%async_computation.8 | async-start | bytes 1996800 | tf_op jit(solution)/shard_map/all_gather | solution.py:106
  12.6 88.3 %copy-start.6 = (bf16[1,3,64,1280]{3,2,1,0:T(8,128)(2,1)S(1)}, bf16[1,3,64,1280]{3,2,1,0:T(8,128)(2,1)}, u32[]{:S(2)}) copy-start(bf16[1,3,64,1280]{3,2,1,0:T(8,128)(2,1)} %param.10) | copy-start | bytes 1474564
  101.0 8.4 %copy-start.3 = (bf16[1,3,64,1280]{3,2,1,0:T(8,128)(2,1)S(1)}, bf16[1,3,64,1280]{3,2,1,0:T(8,128)(2,1)}, u32[]{:S(2)}) copy-start(bf16[1,3,64,1280]{3,2,1,0:T(8,128)(2,1)} %param.8) | copy-start | bytes 1474564
  101.0 8.4 copy-start.14
  102.6 83.2 %all-to-all-start.4 = ((bf16[3,64,640]{2,0,1:T(4,128)(2,1)}), bf16[3,64,640]{2,0,1:T(4,128)(2,1)S(1)}, u32[]{:S(2)}, u32[]{:S(2)}) async-start(bf16[3,64,640]{2,0,1:T(4,128)(2,1)} %copy.52), calls=%async_computation.4 | async-start | bytes 655360 | tf_op jit(solution)/shard_map/all_to_all | solution.py:146
  110.7 73.6 %copy-start.5 = (bf16[192,1280]{1,0:T(8,128)(2,1)}, bf16[192,1280]{1,0:T(8,128)(2,1)S(1)}, u32[]{:S(2)}) copy-start(bf16[192,1280]{1,0:T(8,128)(2,1)S(1)} %get-tuple-element.6) | copy-start | bytes 1474564
  185.9 7.1 copy-start.11
  185.9 84.8 %all-to-all-start.2 = ((bf16[3,64,640]{2,0,1:T(4,128)(2,1)}), bf16[3,64,640]{2,0,1:T(4,128)(2,1)}, u32[]{:S(2)}, u32[]{:S(2)}) async-start(bf16[3,64,640]{2,0,1:T(4,128)(2,1)} %copy.45), calls=%async_computation.2 | async-start | bytes 655360 | tf_op jit(solution)/shard_map/all_to_all | solution.py:123
  270.7 93.7 %all-to-all-start.1 = ((bf16[3,64,640]{2,0,1:T(4,128)(2,1)}), bf16[3,64,640]{2,0,1:T(4,128)(2,1)}, u32[]{:S(2)}, u32[]{:S(2)}) async-start(bf16[3,64,640]{2,0,1:T(4,128)(2,1)} %copy.44), calls=%async_computation.1 | async-start | bytes 655360 | tf_op jit(solution)/shard_map/all_to_all | solution.py:122
  364.3 23.6 %all-to-all-start = ((bf16[3,64,640]{2,0,1:T(4,128)(2,1)}), bf16[3,64,640]{2,0,1:T(4,128)(2,1)}, u32[]{:S(2)}, u32[]{:S(2)}) async-start(bf16[3,64,640]{2,0,1:T(4,128)(2,1)} %copy.43), calls=%async_computation | async-start | bytes 655360 | tf_op jit(solution)/shard_map/all_to_all | solution.py:124
  387.9 23.7 %all-to-all-start.7 = ((bf16[64,2,960]{2,1,0:T(2,128)(2,1)}), bf16[64,2,960]{2,1,0:T(2,128)(2,1)}, u32[]{:S(2)}, u32[]{:S(2)}) async-start(bf16[64,2,960]{2,1,0:T(2,128)(2,1)} %reshape.332), calls=%async_computation.7 | async-start | bytes 524288 | tf_op jit(solution)/shard_map/all_to_all | solution.py:153
  411.6 23.8 %all-to-all-start.3 = ((bf16[64,2,960]{2,1,0:T(2,128)(2,1)}), bf16[64,2,960]{2,1,0:T(2,128)(2,1)}, u32[]{:S(2)}, u32[]{:S(2)}) async-start(bf16[64,2,960]{2,1,0:T(2,128)(2,1)} %reshape.326), calls=%async_computation.3 | async-start | bytes 524288 | tf_op jit(solution)/shard_map/all_to_all | solution.py:127
  435.3 41.9 %all-to-all-start.6 = ((bf16[64,2,960]{2,1,0:T(2,128)(2,1)}), bf16[64,2,960]{2,1,0:T(2,128)(2,1)}, u32[]{:S(2)}, u32[]{:S(2)}) async-start(bf16[64,2,960]{2,1,0:T(2,128)(2,1)} %reshape.330), calls=%async_computation.6 | async-start | bytes 524288 | tf_op jit(solution)/shard_map/all_to_all | solution.py:152
  477.2 25.3 %all-to-all-start.5 = ((bf16[64,2,960]{2,1,0:T(2,128)(2,1)}), bf16[64,2,960]{2,1,0:T(2,128)(2,1)}, u32[]{:S(2)}, u32[]{:S(2)}) async-start(bf16[64,2,960]{2,1,0:T(2,128)(2,1)} %reshape.328), calls=%async_computation.5 | async-start | bytes 524288 | tf_op jit(solution)/shard_map/all_to_all | solution.py:151
  497.1 3.0 copy-start.7
  497.1 3.0 copy-start.10
  512.1 1.7 copy-start.9
  512.1 1.7 copy-start.12
  514.9 314.9 %copy-start.4 = (bf16[1,3,64,1280]{3,2,1,0:T(8,128)(2,1)S(1)}, bf16[1,3,64,1280]{3,2,1,0:T(8,128)(2,1)}, u32[]{:S(2)}) copy-start(bf16[1,3,64,1280]{3,2,1,0:T(8,128)(2,1)} %param.8) | copy-start | bytes 1474564
  514.9 314.9 %copy-start.8 = (bf16[1,3,64,1280]{3,2,1,0:T(8,128)(2,1)S(1)}, bf16[1,3,64,1280]{3,2,1,0:T(8,128)(2,1)}, u32[]{:S(2)}) copy-start(bf16[1,3,64,1280]{3,2,1,0:T(8,128)(2,1)} %param.10) | copy-start | bytes 1474564
  (3 other events, 4.0 us)
Sparse Core Ops, SparseCore 0:
  11.3 86.8 all-gather.16
  101.5 80.3 all-gather.14
  185.2 80.4 all-gather.12
  268.8 80.4 all-gather.10
